TPU v7x, 32 devices: a whole 2x2x4 slice. The times are simulated.
32 devices in a mesh: dp: 8 (over z, y), tensor: 4 (over x, core).
Axes of the slice: x: 2, y: 2, z: 4, core: 2. Of those that a mesh axis runs over, the one named last changes fastest.
Arguments:
- tokens: bfloat16 [16384, 1024], P(('dp', 'tensor')), may hold values from -6 to 6
- ln_gain: float32 [1024], replicated, may hold values from 0.1 to 1.9
- ln_bias: float32 [1024], replicated, may hold values from -1.75 to 1.75
- w_qkv: bfloat16 [3, 1024, 16, 64], P(None, None, 'tensor'), may hold values from -0.1875 to 0.1875
- b_qkv: float32 [3, 16, 64], P(None, 'tensor'), may hold values from -3 to 3
- w_in: bfloat16 [1024, 4096], P(None, 'tensor'), may hold values from -0.1875 to 0.1875
- b_in: float32 [4096], P('tensor'), may hold values from -3 to 3
- w_out: bfloat16 [16, 64, 1024], P('tensor'), may hold values from -1.5 to 1.5
- w_down: bfloat16 [4096, 1024], P('tensor'), may hold values from -0.09375 to 0.09375
- b_out: float32 [1024], replicated, may hold values from -3 to 3
- cotangent: bfloat16 [16384, 1024], P(('dp', 'tensor')), may hold values from -6 to 6
- block_doc: int32 [8, 4], P('dp'), may hold values from 0 to 2, as said below
Outputs:
- block_out: bfloat16 [16384, 1024], P(('dp', 'tensor'))
- grad_tokens: float32 [16384, 1024], P(('dp', 'tensor'))
- grad_ln_gain: float32 [1024], replicated
- grad_ln_bias: float32 [1024], replicated
- grad_w_qkv: float32 [3, 1024, 16, 64], P(None, 'dp', 'tensor')
- grad_b_qkv: float32 [3, 16, 64], replicated
- grad_w_in: float32 [1024, 4096], P('dp', 'tensor')
- grad_b_in: float32 [4096], replicated
- grad_w_out: float32 [16, 64, 1024], P('tensor', None, 'dp')
- grad_w_down: float32 [4096, 1024], P('tensor', 'dp')
- grad_b_out: float32 [1024], replicated
Inputs may be any that keep to these rules, and one draw needn't show every extreme that they name: `block_doc`: in each group the numbers start at 0 and rise by 0 or 1 from block to block. Every sequence covers a power of two of blocks, at most 2; a sequence of k blocks starts at a block index divisible by k; each group has a sequence of exactly 2 blocks.
All inputs are finite; a program needn't handle non-finite values.
Results may differ from a plain program's by a relative error of at most 0.012.
The roundings to bfloat16 on the way count: a program that leaves them out, or rounds other values in their place, can miss the bound.
Values may be sent and summed in bfloat16 or wider, within the bound.
No kernel may reach another device: no remote copies, remote signals or barrier semaphores. Data moves between devices by JAX's collectives and lax.ppermute only.
A program may use at most 256 MiB of HBM per device.

v0:
```python
from functools import partial
import jax
import jax.numpy as jnp
from jax import lax
from jax.sharding import PartitionSpec as P

HEADS = 16
FF = 4096
ROT = 16
BLK = 512
epsilon = 1e-05


def layer_norm(rows, ln_gain, ln_bias):
    mean_row = jnp.mean(rows, axis=-1, keepdims=True)
    centred = rows - mean_row
    var_row = jnp.mean(centred * centred, axis=-1, keepdims=True)
    return centred * lax.rsqrt(var_row + epsilon) * ln_gain + ln_bias


def rope_tables(positions):
    half_dims = ROT // 2
    inverse = 1.0 / 10000.0 ** (jnp.arange(half_dims, dtype=jnp.float32) * 2.0 / ROT)
    angles = positions[:, None] * inverse[None, :]
    return (jnp.cos(angles), jnp.sin(angles))


def rotate(vectors, cosine_table, sine_table):
    half_dims = ROT // 2
    leading = vectors[..., :half_dims]
    trailing = vectors[..., half_dims:ROT]
    remain = vectors[..., ROT:]
    cosine = cosine_table[:, None, :]
    sine = sine_table[:, None, :]
    return jnp.concatenate(
        [leading * cosine - trailing * sine, trailing * cosine + leading * sine, remain], axis=-1
    )


def shards(
    tokens, ln_gain, ln_bias, w_qkv, b_qkv, w_in, b_in, w_out, w_down, b_out, cotangent, block_doc
):
    rows_local = tokens.shape[0]
    model_width = tokens.shape[1]
    heads_local = w_qkv.shape[2]
    head_dim = w_qkv.shape[3]
    attn_cols = heads_local * head_dim
    hidden_local = w_in.shape[1]
    score_scale = head_dim ** (-0.5)
    token_values = tokens.astype(jnp.float32)
    normed_rows, ln_back = jax.vjp(layer_norm, token_values, ln_gain, ln_bias)
    normed_low = normed_rows.astype(jnp.bfloat16)
    gathered = lax.all_gather(normed_low, "tensor", axis=0, tiled=True)
    group_rows = gathered.shape[0]
    num_blocks = group_rows // BLK
    seq_blocks = min(4, num_blocks // 2)
    window = seq_blocks * BLK
    pad_rows = window - BLK
    joined_weight = jnp.concatenate(
        [
            w_qkv[0].reshape(model_width, attn_cols),
            w_qkv[1].reshape(model_width, attn_cols),
            w_qkv[2].reshape(model_width, attn_cols),
            w_in,
        ],
        axis=1,
    )
    joined_bias = jnp.concatenate([b_qkv.reshape(3 * attn_cols), b_in])
    upward = jnp.dot(gathered, joined_weight, preferred_element_type=jnp.float32) + joined_bias
    query_pre = upward[:, :attn_cols].reshape(group_rows, heads_local, head_dim)
    key_pre = upward[:, attn_cols : 2 * attn_cols].reshape(group_rows, heads_local, head_dim)
    value_pre = upward[:, 2 * attn_cols : 3 * attn_cols].reshape(group_rows, heads_local, head_dim)
    hidden_pre = upward[:, 3 * attn_cols :]
    sequence_ids = block_doc[0]
    block_starts = jnp.sum(
        (sequence_ids[None, :] < sequence_ids[:, None]).astype(jnp.int32), axis=1
    )
    positions = (
        jnp.arange(group_rows, dtype=jnp.int32) - jnp.repeat(block_starts, BLK) * BLK
    ).astype(jnp.float32)
    cosine_table, sine_table = rope_tables(positions)
    all_queries = rotate(query_pre, cosine_table, sine_table).astype(jnp.bfloat16)
    all_keys = rotate(key_pre, cosine_table, sine_table).astype(jnp.bfloat16)
    all_values = value_pre.astype(jnp.bfloat16)
    pad_heads = jnp.zeros((pad_rows, heads_local, head_dim), jnp.bfloat16)
    keys_padded = jnp.concatenate([pad_heads, all_keys], axis=0)
    values_padded = jnp.concatenate([pad_heads, all_values], axis=0)
    padded_docs = jnp.concatenate([jnp.full((seq_blocks - 1,), -1, jnp.int32), sequence_ids])
    key_docs = jnp.repeat(padded_docs, BLK)
    query_offset = lax.broadcasted_iota(jnp.int32, (BLK, window), 0)
    key_offset = lax.broadcasted_iota(jnp.int32, (BLK, window), 1)
    causal = key_offset - pad_rows <= query_offset

    def window_scores(query_block):
        first_row = query_block * BLK
        query_rows = lax.dynamic_slice_in_dim(all_queries, first_row, BLK, 0)
        key_rows = lax.dynamic_slice_in_dim(keys_padded, first_row, window, 0)
        value_rows = lax.dynamic_slice_in_dim(values_padded, first_row, window, 0)
        window_docs = lax.dynamic_slice_in_dim(key_docs, first_row, window, 0)
        allowed = (window_docs[None, :] == sequence_ids[query_block]) & causal
        scores = (
            jnp.einsum("qhe,khe->hqk", query_rows, key_rows, preferred_element_type=jnp.float32)
            * score_scale
        )
        return (query_rows, key_rows, value_rows, jnp.where(allowed[None], scores, -1e30))

    def attend(query_block):
        query_rows, key_rows, value_rows, scores = window_scores(query_block)
        maxima = jnp.max(scores, axis=-1)
        log_total = maxima + jnp.log(jnp.sum(jnp.exp(scores - maxima[..., None]), axis=-1))
        weights = jax.nn.softmax(scores, axis=-1).astype(jnp.bfloat16)
        out_rows = jnp.einsum(
            "hqk,khe->qhe", weights, value_rows, preferred_element_type=jnp.float32
        )
        return (out_rows, log_total)

    attended_blocks, log_totals = lax.map(attend, jnp.arange(num_blocks, dtype=jnp.int32))
    attended = attended_blocks.reshape(group_rows, attn_cols).astype(jnp.bfloat16)
    w_out_flat = w_out.reshape(attn_cols, model_width)
    active_full, gelu_back = jax.vjp(partial(jax.nn.gelu, approximate=False), hidden_pre)
    active = active_full.astype(jnp.bfloat16)
    active_rows = lax.dynamic_slice_in_dim(
        active, jnp.int32(0), rows_local * lax.axis_size("tensor"), 0
    )
    mixed = lax.psum_scatter(
        jnp.dot(attended, w_out_flat, preferred_element_type=jnp.float32)
        + jnp.dot(active_rows, w_down, preferred_element_type=jnp.float32),
        "tensor",
        scatter_dimension=0,
        tiled=True,
    )
    block_out = (token_values + mixed + b_out).astype(jnp.bfloat16)
    cotangent_group = lax.all_gather(cotangent, "tensor", axis=0, tiled=True)
    grad_attended = jnp.einsum(
        "td,cd->tc", cotangent_group, w_out_flat, preferred_element_type=jnp.float32
    ).astype(jnp.bfloat16)
    grad_active = jnp.einsum(
        "td,fd->tf", cotangent_group, w_down, preferred_element_type=jnp.float32
    )
    grad_w_out = jnp.einsum(
        "tc,td->cd", attended, cotangent_group, preferred_element_type=jnp.float32
    )
    grad_w_down = jnp.einsum(
        "tf,td->fd", active, cotangent_group, preferred_element_type=jnp.float32
    )
    grad_hidden = gelu_back(grad_active)[0].astype(jnp.bfloat16)
    grad_out_heads = grad_attended.reshape(group_rows, heads_local, head_dim)

    def back_block(query_block, carried):
        grad_q_all, grad_k_padded, grad_v_padded = carried
        first_row = query_block * BLK
        query_rows, key_rows, value_rows, scores = window_scores(query_block)
        grad_rows_out = lax.dynamic_slice_in_dim(grad_out_heads, first_row, BLK, 0)
        weights = jnp.exp(scores - log_totals[query_block][..., None])
        grad_weights = jnp.einsum(
            "qhe,khe->hqk", grad_rows_out, value_rows, preferred_element_type=jnp.float32
        )
        deltas = jnp.sum(weights * grad_weights, axis=-1)
        grad_scores = (weights * (grad_weights - deltas[..., None])).astype(jnp.bfloat16)
        grad_q_rows = (
            jnp.einsum("hqk,khe->qhe", grad_scores, key_rows, preferred_element_type=jnp.float32)
            * score_scale
        )
        grad_k_rows = (
            jnp.einsum("hqk,qhe->khe", grad_scores, query_rows, preferred_element_type=jnp.float32)
            * score_scale
        )
        grad_v_rows = jnp.einsum(
            "hqk,qhe->khe",
            weights.astype(jnp.bfloat16),
            grad_rows_out,
            preferred_element_type=jnp.float32,
        )
        old_k = lax.dynamic_slice_in_dim(grad_k_padded, first_row, window, 0)
        old_v = lax.dynamic_slice_in_dim(grad_v_padded, first_row, window, 0)
        grad_k_padded = lax.dynamic_update_slice_in_dim(
            grad_k_padded, old_k + grad_k_rows, first_row, 0
        )
        grad_v_padded = lax.dynamic_update_slice_in_dim(
            grad_v_padded, old_v + grad_v_rows, first_row, 0
        )
        grad_q_all = lax.dynamic_update_slice_in_dim(grad_q_all, grad_q_rows, first_row, 0)
        return (grad_q_all, grad_k_padded, grad_v_padded)

    zero_heads = jnp.zeros((group_rows, heads_local, head_dim), jnp.float32)
    zero_padded = jnp.zeros((group_rows + pad_rows, heads_local, head_dim), jnp.float32)
    grad_queries, grad_k_padded, grad_v_padded = lax.fori_loop(
        0, num_blocks, back_block, (zero_heads, zero_padded, zero_padded)
    )
    grad_keys = grad_k_padded[pad_rows:]
    grad_values = grad_v_padded[pad_rows:]
    grad_q_pre = (
        rotate(grad_queries, cosine_table, -sine_table)
        .astype(jnp.bfloat16)
        .reshape(group_rows, attn_cols)
    )
    grad_k_pre = (
        rotate(grad_keys, cosine_table, -sine_table)
        .astype(jnp.bfloat16)
        .reshape(group_rows, attn_cols)
    )
    grad_v_pre = grad_values.astype(jnp.bfloat16).reshape(group_rows, attn_cols)
    grad_upward = jnp.concatenate([grad_q_pre, grad_k_pre, grad_v_pre, grad_hidden], axis=1)
    grad_joined_weight = jnp.einsum(
        "td,tc->dc", gathered, grad_upward, preferred_element_type=jnp.float32
    )
    grad_joined_bias = jnp.sum(grad_upward, axis=0, dtype=jnp.float32)
    grad_normed = lax.psum_scatter(
        jnp.einsum("tc,dc->td", grad_upward, joined_weight, preferred_element_type=jnp.float32),
        "tensor",
        scatter_dimension=0,
        tiled=True,
    )
    grad_tokens_norm, grad_gain_part, grad_bias_part = ln_back(grad_normed)
    grad_tokens = grad_tokens_norm + cotangent.astype(jnp.float32)
    grad_bout_part = jnp.sum(cotangent, axis=0, dtype=jnp.float32)
    grad_w_qkv_local = jnp.stack(
        [
            grad_joined_weight[:, member * attn_cols : (member + 1) * attn_cols].reshape(
                model_width, heads_local, head_dim
            )
            for member in range(3)
        ]
    )
    grad_w_in_local = grad_joined_weight[:, 3 * attn_cols :]
    tensor_rank = lax.axis_index("tensor")
    bqkv_full = lax.dynamic_update_slice(
        jnp.zeros((3, HEADS, head_dim), jnp.float32),
        grad_joined_bias[: 3 * attn_cols].reshape(3, heads_local, head_dim),
        (jnp.int32(0), tensor_rank * heads_local, jnp.int32(0)),
    )
    bin_full = lax.dynamic_update_slice(
        jnp.zeros((FF,), jnp.float32),
        grad_joined_bias[3 * attn_cols :],
        (tensor_rank * hidden_local,),
    )
    grad_ln_gain, grad_ln_bias, grad_b_out, grad_b_qkv, grad_b_in = lax.psum(
        (grad_gain_part, grad_bias_part, grad_bout_part, bqkv_full, bin_full), ("dp", "tensor")
    )
    grad_w_qkv, grad_w_in, grad_w_out_part, grad_w_down_part = (
        lax.psum_scatter(grad_w_qkv_local, "dp", scatter_dimension=1, tiled=True),
        lax.psum_scatter(grad_w_in_local, "dp", scatter_dimension=0, tiled=True),
        lax.psum_scatter(
            grad_w_out.reshape(heads_local, head_dim, model_width),
            "dp",
            scatter_dimension=2,
            tiled=True,
        ),
        lax.psum_scatter(grad_w_down, "dp", scatter_dimension=1, tiled=True),
    )
    return (
        block_out,
        grad_tokens,
        grad_ln_gain,
        grad_ln_bias,
        grad_w_qkv,
        grad_b_qkv,
        grad_w_in,
        grad_b_in,
        grad_w_out_part,
        grad_w_down_part,
        grad_b_out,
    )


def solution(mesh):
    return jax.shard_map(
        shards,
        mesh=mesh,
        in_specs=(
            P(("dp", "tensor"), None),
            P(),
            P(),
            P(None, None, "tensor", None),
            P(None, "tensor", None),
            P(None, "tensor"),
            P("tensor"),
            P("tensor", None, None),
            P("tensor", None),
            P(),
            P(("dp", "tensor"), None),
            P("dp", None),
        ),
        out_specs=(
            P(("dp", "tensor"), None),
            P(("dp", "tensor"), None),
            P(),
            P(),
            P(None, "dp", "tensor", None),
            P(),
            P("dp", "tensor"),
            P(),
            P("tensor", None, "dp"),
            P("tensor", "dp"),
            P(),
        ),
        check_vma=False,
    )
```

profile of v0, /device:TPU:0, one launch (start us, length us, event | category | flops | bytes accessed | tf_op | source)
XLA Modules:
  0.0 755.2 jit_solution(2105448763767745747)
XLA Ops:
  11.7 2.7 fusion.71
  22.3 29.4 %all-gather.3.cloned.1.call-done = bf16[2048,1024]{1,0:T(8,128)(2,1)} async-done(((bf16[512,1024]{1,0:T(8,128)(2,1)}), bf16[2048,1024]{1,0:T(8,128)(2,1)}) %all-gather.3.cloned.1.call-update) | async-done | bytes 4194320 | tf_op jit(solution)/shard_map/all_gather | solution.py:53
  51.7 14.2 %convolution_add_fusion = f32[2048,1792]{0,1:T(8,128)} fusion(bf16[2048,1024]{1,0:T(8,128)(2,1)} %all-gather.3.cloned.1.call-done, f32[1792]{0:T(1024)S(1)} %pad_maximum_fusion.8, bf16[1024,1024]{1,0:T(8,128)(2,1)} %param.21, bf16[1024,256]{1,0:T(8,128)(2,1)S(1)} %copy.38, bf16[1024,256]{1,0:T(8,128)(2,1)} %copy.37, bf16[1024,256]{1,0:T(8,128)(2,1)} %copy.36), kind=kOutput, calls=%fused_computation.77 | convolution fusion | flops 7534542848 | bytes 22551552 | tf_op jit(solution)/shard_map/dot_general | solution.py:69
  65.9 2.5 fusion.88
  74.0 59.7 %while.31 = (s32[]{:T(128)}, bf16[4,512,4,64]{1,3,2,0:T(8,128)(2,1)}, f32[4,4,512]{2,1,0:T(4,128)}, s32[4]{0:T(128)S(1)}, bf16[2560,4,64]{0,2,1:T(8,128)(2,1)}, ...) while((s32[]{:T(128)}, ...), condition=%wide.region_6.7_spmd.clone, body=%wide.region_3.6_spmd.clone.sunk | while | flops 563084288 | bytes 29175080 | solution.py:117
  78.9 2.8 fusion.128
  84.7 4.3 fusion.130
  93.9 2.8 fusion.128
  99.6 4.3 fusion.130
  108.8 2.8 fusion.128
  114.5 4.3 fusion.130
  123.7 2.8 fusion.128
  129.5 4.3 fusion.130
  133.8 4.7 convolution_convert_fusion
  143.6 80.2 %while.32 = (s32[]{:T(128)}, f32[2048,4,64]{0,2,1:T(8,128)}, f32[2560,4,64]{0,2,1:T(8,128)}, f32[2560,4,64]{0,2,1:T(8,128)}, bf16[2560,4,64]{0,2,1:T(8,128)(2,1)...) while((s32[]{:T(128)}, f32[2048,4,64]{0,2,1:T(8,128)}, ...), condition=%wide.region_10.11_spmd.clone, body=%wide.region_8.10_spmd.clone.sunk | while | flops 1375599616 | bytes 97585616 | solution.py:187
  148.6 4.2 multiply_reduce_fusion.2
  152.8 2.4 multiply_convert_fusion.3
  159.4 4.5 fusion.143
  168.6 4.2 multiply_reduce_fusion.2
  172.8 2.4 multiply_convert_fusion.3
  179.4 4.5 fusion.143
  188.6 4.2 multiply_reduce_fusion.2
  192.8 2.4 multiply_convert_fusion.3
  199.3 4.5 fusion.143
  208.6 4.2 multiply_reduce_fusion.2
  219.3 4.5 fusion.143
  230.4 26.7 %add_convert_fusion = (bf16[2048,1024]{0,1:T(8,128)(2,1)S(1)}, f32[2048,1024]{0,1:T(8,128)}) fusion(f32[2048,1792]{0,1:T(8,128)} %convolution_add_fusion, bf16[2048,1024]{1,0:T(8,128)(2,1)S(1)} %copy-done.29, bf16[1024,1024]{1,0:T(8,128)(2,1)S(1)} %copy-done), kind=kOutput, calls=%fused_computation.61 | convolution fusion | flops 4445962240 | bytes 27262976 | tf_op jit(solution)/shard_map/td,fd->tf/dot_general | solution.py:137
  259.2 12.7 %fusion.79 = f32[2048,1024]{1,0:T(8,128)} fusion(bf16[1024,1024]{1,0:T(8,128)(2,1)} %param.21, bf16[1024,256]{1,0:T(8,128)(2,1)S(1)} %copy-done.17, bf16[1024,256]{1,0:T(8,128)(2,1)S(1)} %copy-done.15, bf16[1024,256]{1,0:T(8,128)(2,1)S(1)} %copy-done.14, bf16[2048,1024]{0,1:T(8,128)(2,1)S(1)} %get-tuple-element.373, bf16[2048,256]{0,1:T(8,128)(2,1)S(1)} %bitcast.104, ...), kind=kOutput, calls=%fused_computation.119 | convolution fusion | flops 7560232960 | bytes 19398656 | tf_op jit(solution)/shard_map/tc,dc->td/dot_general | solution.py:209
  274.4 11.8 %multiply_convert_fusion.1 = bf16[2048,1024]{0,1:T(8,128)(2,1)} fusion(f32[2048,1024]{0,1:T(8,128)} %get-tuple-element.374, f32[2048,1792]{0,1:T(8,128)} %convolution_add_fusion), kind=kLoop, calls=%fused_computation.62 | loop fusion | flops 6291456 | bytes 20971520 | tf_op jit(solution)/shard_map/convert_element_type | solution.py:121
  286.2 6.6 fusion.91
  292.8 4.8 convolution_add_fusion.1
  297.7 4.4 fusion.59
  302.4 12.4 %fusion.85 = f32[1024,1792]{1,0:T(8,128)S(1)} fusion(bf16[2048,1024]{1,0:T(8,128)(2,1)} %all-gather.3.cloned.1.call-done, bf16[2048,1024]{0,1:T(8,128)(2,1)} %copy-done.6, bf16[2048,256]{0,1:T(8,128)(2,1)} %bitcast.105, bf16[2048,256]{0,1:T(8,128)(2,1)} %bitcast.114, bf16[2048,256]{0,1:T(8,128)(2,1)} %bitcast.111), kind=kOutput, calls=%fused_computation.149 | convolution fusion | flops 7545552896 | bytes 18874368 | tf_op jit(solution)/shard_map/td,tc->dc/dot_general | solution.py:204
  314.7 3.0 copy-done.5
  321.0 2.7 copy.41
  323.7 2.6 copy.42
  326.3 3.6 pad_maximum_fusion.2
  330.0 4.8 slice.139
  335.1 10.1 %fusion.92 = f32[1024,1024]{1,0:T(8,128)} fusion(bf16[2048,1024]{0,1:T(8,128)(2,1)} %multiply_convert_fusion.1, bf16[2048,1024]{1,0:T(8,128)(2,1)} %all-gather.5.cloned.1.call-done), kind=kOutput, calls=%fused_computation.155 | convolution fusion | flops 4294967296 | bytes 12582912 | tf_op jit(solution)/shard_map/tf,td->fd/dot_general | solution.py:143
  345.2 4.3 convert_reduce_fusion
  351.9 2.6 fusion.72
  354.4 63.1 %reduce-scatter.7.cloned.1.call-done = f32[512,1024]{1,0:T(8,128)} async-done(((f32[2048,1024]{1,0:T(8,128)}), f32[512,1024]{1,0:T(8,128)}) %reduce-scatter.7.cloned.1.call-update) | async-done | bytes 2097168 | tf_op jit(solution)/shard_map/reduce_scatter | solution.py:125
  417.5 5.1 convert_reduce_fusion.2
  422.7 40.9 %all-reduce.2 = (f32[1024]{0:T(1024)}, f32[1024]{0:T(1024)}, f32[3,16,64]{2,1,0:T(8,128)}, f32[4096]{0:T(1024)}, f32[1024]{0:T(1024)}) all-reduce(f32[1024]{0:T(1024)S(1)} %get-tuple-element.320, f32[1024]{0:T(1024)S(1)} %get-tuple-element.322, ...), channel_id=1, replica_groups=mesh['dp'=8,'tensor'=4] {'dp','tensor'}, use_global_device_ids=true, to_apply=%region_15.16 | all-reduce | flops 10240 | bytes 81920 | tf_op jit(solution)/shard_map/psum | solution.py:237
  463.6 22.5 %reduce-scatter.15.cloned.1.call-done = f32[4,64,128]{2,1,0:T(8,128)} async-done(((f32[4,64,1024]{2,1,0:T(8,128)}), f32[4,64,128]{2,1,0:T(8,128)}) %reduce-scatter.15.cloned.1.call-update) | async-done | bytes 131088 | tf_op jit(solution)/shard_map/reduce_scatter | solution.py:243
  486.1 77.8 %reduce-scatter.11.cloned.1.call-done = f32[3,128,4,64]{1,3,2,0:T(8,128)} async-done(((f32[3,1024,4,64]{1,3,2,0:T(8,128)}), f32[3,128,4,64]{1,3,2,0:T(8,128)}) %reduce-scatter.11.cloned.1.call-update) | async-done | bytes 393232 | tf_op jit(solution)/shard_map/reduce_scatter | solution.py:241
  563.8 91.7 %reduce-scatter.13.cloned.1.call-done = f32[128,1024]{1,0:T(8,128)} async-done(((f32[1024,1024]{1,0:T(8,128)}), f32[128,1024]{1,0:T(8,128)}) %reduce-scatter.13.cloned.1.call-update) | async-done | bytes 524304 | tf_op jit(solution)/shard_map/reduce_scatter | solution.py:242
  655.5 92.6 %reduce-scatter.17.cloned.1.call-done = f32[1024,128]{1,0:T(8,128)} async-done(((f32[1024,1024]{1,0:T(8,128)}), f32[1024,128]{1,0:T(8,128)}) %reduce-scatter.17.cloned.1.call-update) | async-done | bytes 524304 | tf_op jit(solution)/shard_map/reduce_scatter | solution.py:249
  (210 shorter events, 99.2 us)
Async XLA Ops:
  7.2 223.1 %copy-start = (bf16[1024,1024]{1,0:T(8,128)(2,1)S(1)}, bf16[1024,1024]{1,0:T(8,128)(2,1)}, u32[]{:S(2)}) copy-start(bf16[1024,1024]{1,0:T(8,128)(2,1)} %param.24) | copy-start | bytes 6291460
  7.2 13.6 %copy-start.26 = (f32[3,4,64]{2,1,0:T(4,128)S(1)}, f32[3,4,64]{2,1,0:T(4,128)}, u32[]{:S(2)}) copy-start(f32[3,4,64]{2,1,0:T(4,128)} %param.20) | copy-start | bytes 9220
  7.2 13.7 %copy-start.30 = (s32[1,4]{1,0:T(1,128)S(1)}, s32[1,4]{1,0:T(1,128)}, u32[]{:S(2)}) copy-start(s32[1,4]{1,0:T(1,128)} %param.27) | copy-start | bytes 52
  7.2 14.1 %copy-start.28 = (f32[1024]{0:T(1024)S(1)}, f32[1024]{0:T(1024)}, u32[]{:S(2)}) copy-start(f32[1024]{0:T(1024)} %param.22) | copy-start | bytes 12292
  7.2 44.5 %all-gather.3.cloned.1.call-start = ((), (), s32[]{:S(2)}) async-start(), calls=%async_computation.6 | async-start | bytes 5242880 | tf_op jit(solution)/shard_map/all_gather | solution.py:53
  8.8 2.2 copy-start.19
  14.4 119.4 %all-gather.5.cloned.1.call-start = ((), (), s32[]{:S(2)}) async-start(), calls=%async_computation.8 | async-start | bytes 5242880 | tf_op jit(solution)/shard_map/all_gather | solution.py:133
  15.1 334.6 %reduce-scatter.9.cloned.1.call-start = ((), (), s32[]{:S(2)}) async-start(), calls=%async_computation.9 | async-start | bytes 10485760 | tf_op jit(solution)/shard_map/reduce_scatter | solution.py:208
  20.8 45.1 %copy-start.16 = (bf16[1024,256]{1,0:T(8,128)(2,1)}, bf16[1024,256]{1,0:T(8,128)(2,1)S(1)}, u32[]{:S(2)}) copy-start(bf16[1024,256]{1,0:T(8,128)(2,1)S(1)} %copy.38) | copy-start | bytes 1572868
  22.3 48.1 %copy-start.11 = (f32[2048,8]{0,1:T(8,128)}, f32[2048,8]{0,1:T(8,128)S(1)}, u32[]{:S(2)}) copy-start(f32[2048,8]{0,1:T(8,128)S(1)} %get-tuple-element.404) | copy-start | bytes 196612
  133.8 9.9 %copy-start.1 = (bf16[2560,4,64]{0,2,1:T(8,128)(2,1)S(1)}, bf16[2560,4,64]{0,2,1:T(8,128)(2,1)}, u32[]{:S(2)}) copy-start(bf16[2560,4,64]{0,2,1:T(8,128)(2,1)} %get-tuple-element.658) | copy-start | bytes 3932164
  143.6 83.4 %copy-start.12 = (f32[2048,8]{0,1:T(8,128)S(1)}, f32[2048,8]{0,1:T(8,128)}, u32[]{:S(2)}) copy-start(f32[2048,8]{0,1:T(8,128)} %copy-done.11) | copy-start | bytes 196612
  143.6 83.4 %copy-start.18 = (f32[2048,8]{0,1:T(8,128)S(1)}, f32[2048,8]{0,1:T(8,128)}, u32[]{:S(2)}) copy-start(f32[2048,8]{0,1:T(8,128)} %get-tuple-element.402) | copy-start | bytes 196612
  143.9 2.4 copy-start.31
  143.9 4.8 copy-start.10
  152.8 2.4 copy-start.3
  163.9 2.3 copy-start.31
  163.9 4.7 copy-start.10
  172.8 2.4 copy-start.3
  177.2 2.2 copy-start.4
  183.8 2.3 copy-start.31
  183.8 4.7 copy-start.10
  192.8 2.4 copy-start.3
  197.1 2.2 copy-start.4
  203.8 2.3 copy-start.31
  203.8 4.7 copy-start.10
  212.8 2.4 copy-start.3
  217.1 2.2 copy-start.4
  223.8 6.5 copy-start.29
  230.2 27.0 %copy-start.7 = (bf16[2048,4,64]{0,2,1:T(8,128)(2,1)}, bf16[2048,4,64]{0,2,1:T(8,128)(2,1)S(1)}, u32[]{:S(2)}) copy-start(bf16[2048,4,64]{0,2,1:T(8,128)(2,1)S(1)} %slice.174) | copy-start | bytes 3145732
  230.3 26.8 %copy-start.8 = (bf16[2048,4,64]{0,2,1:T(8,128)(2,1)}, bf16[2048,4,64]{0,2,1:T(8,128)(2,1)S(1)}, u32[]{:S(2)}) copy-start(bf16[2048,4,64]{0,2,1:T(8,128)(2,1)S(1)} %get-tuple-element.405) | copy-start | bytes 3145732
  230.4 26.8 %copy-start.9 = (bf16[2048,4,64]{0,2,1:T(8,128)(2,1)}, bf16[2048,4,64]{0,2,1:T(8,128)(2,1)S(1)}, u32[]{:S(2)}) copy-start(bf16[2048,4,64]{0,2,1:T(8,128)(2,1)S(1)} %get-tuple-element.406) | copy-start | bytes 3145732
  230.4 28.8 %copy-start.14 = (bf16[1024,256]{1,0:T(8,128)(2,1)S(1)}, bf16[1024,256]{1,0:T(8,128)(2,1)}, u32[]{:S(2)}) copy-start(bf16[1024,256]{1,0:T(8,128)(2,1)} %copy.36) | copy-start | bytes 1572868
  230.4 28.8 %copy-start.15 = (bf16[1024,256]{1,0:T(8,128)(2,1)S(1)}, bf16[1024,256]{1,0:T(8,128)(2,1)}, u32[]{:S(2)}) copy-start(bf16[1024,256]{1,0:T(8,128)(2,1)} %copy.37) | copy-start | bytes 1572868
  230.4 28.8 %copy-start.17 = (bf16[1024,256]{1,0:T(8,128)(2,1)S(1)}, bf16[1024,256]{1,0:T(8,128)(2,1)}, u32[]{:S(2)}) copy-start(bf16[1024,256]{1,0:T(8,128)(2,1)} %copy-done.16) | copy-start | bytes 1572868
  271.9 145.6 %reduce-scatter.7.cloned.1.call-start = ((), (), s32[]{:S(2)}) async-start(), calls=%async_computation.7 | async-start | bytes 10485760 | tf_op jit(solution)/shard_map/reduce_scatter | solution.py:125
  286.2 6.6 copy-start.13
  297.6 188.5 %reduce-scatter.15.cloned.1.call-start = ((), (), s32[]{:S(2)}) async-start(), calls=%async_computation.12 | async-start | bytes 1179648 | tf_op jit(solution)/shard_map/reduce_scatter | solution.py:243
  302.1 261.7 %reduce-scatter.11.cloned.1.call-start = ((), (), s32[]{:S(2)}) async-start(), calls=%async_computation.10 | async-start | bytes 3538944 | tf_op jit(solution)/shard_map/reduce_scatter | solution.py:241
  314.7 3.0 copy-start.5
  329.9 325.6 %reduce-scatter.13.cloned.1.call-start = ((), (), s32[]{:S(2)}) async-start(), calls=%async_computation.11 | async-start | bytes 4718592 | tf_op jit(solution)/shard_map/reduce_scatter | solution.py:242
  334.8 413.3 %reduce-scatter.17.cloned.1.call-start = ((), (), s32[]{:S(2)}) async-start(), calls=%async_computation.13 | async-start | bytes 4718592 | tf_op jit(solution)/shard_map/reduce_scatter | solution.py:249
  345.2 4.5 copy-start.2
  345.2 4.5 copy-start.20
  345.2 4.5 copy-start.21
  345.2 6.7 copy-start.25
  345.2 6.7 copy-start.23
  345.2 72.3 %copy-start.27 = (f32[1024]{0:T(1024)S(1)}, f32[1024]{0:T(1024)}, u32[]{:S(2)}) copy-start(f32[1024]{0:T(1024)} %param.25) | copy-start | bytes 12292
  (4 other events, 5.4 us)
Sparse Core Ops, SparseCore 0:
  14.5 37.1 all-gather.2
  53.3 34.5 all-gather.4
  272.0 71.5 reduce-scatter.8
  346.1 71.4 reduce-scatter.6
  421.3 64.6 reduce-scatter.14
  490.1 73.6 reduce-scatter.10
  568.0 87.4 reduce-scatter.12
  659.7 88.3 reduce-scatter.16
where the time goes:
time: 760 us; the launch traced here: 755 us
  waiting for transfers between devices  378 us (50%)
  matrix products  185 us (24%)
  other arithmetic  70.6 us (9%)
  local copies, waits for them, and re-layouts  53.6 us (7%)
  blocking collectives  40.9 us (5%)
  between operations  14.9 us (2%)
  loops' own time  10.9 us (1%)
    reduce_scatter x1, waiting for transfers between devices, shards(): lax.psum_scatter(grad_w_down, 'dp', scatter_dimension=1, tiled=True)  92.6 us
    reduce_scatter x1, waiting for transfers between devices, shards(): lax.psum_scatter(grad_w_in_local, 'dp', scatter_dimension=0, tiled=True)  91.7 us
    reduce_scatter x1, waiting for transfers between devices, shards(): lax.psum_scatter(grad_w_qkv_local, 'dp', scatter_dimension=1, tiled=True)  77.8 us
    reduce_scatter x1, waiting for transfers between devices, shards(): lax.psum_scatter(jnp.dot(attended, w_out_flat, preferred_element_type=jnp...  63.1 us
    psum x1, blocking collectives, shards(): lax.psum((grad_gain_part, grad_bias_part, grad_bout_part, bqkv_full, bin_...  40.9 us
    all_gather x1, waiting for transfers between devices, shards(): gathered = lax.all_gather(normed_low, 'tensor', axis=0, tiled=True)  29.4 us
    dot_general x1, matrix products, shards(): jnp.einsum('td,fd->tf', cotangent_group, w_down, preferred_element_type=j...  26.7 us
    reduce_scatter x1, waiting for transfers between devices, shards(): lax.psum_scatter(grad_w_out.reshape(heads_local, head_dim, model_width),...  22.5 us
  transfers between devices with their start and end apart: 8, of which 6 were waited for; matrix products, arithmetic and copies ran while one was open for 21% of the time, Pallas kernels for 0%

commit v1 on v0

--- a/solution.py
+++ b/solution.py
@@ -50,7 +50,23 @@
     token_values = tokens.astype(jnp.float32)
     normed_rows, ln_back = jax.vjp(layer_norm, token_values, ln_gain, ln_bias)
     normed_low = normed_rows.astype(jnp.bfloat16)
-    gathered = lax.all_gather(normed_low, "tensor", axis=0, tiled=True)
+    ways, here, lap = (lax.axis_size("tensor"), lax.axis_index("tensor"), normed_low.shape[0])
+    dims = [n * ways if d == 0 else n for d, n in enumerate(normed_low.shape)]
+    full = lax.dynamic_update_slice_in_dim(
+        jnp.zeros(dims, normed_low.dtype), normed_low, here * lap, axis=0
+    )
+    going_up = going_down = normed_low
+    for far in range(1, ways // 2 + 1):
+        going_up = lax.ppermute(going_up, "tensor", [(d, (d + 1) % ways) for d in range(ways)])
+        full = lax.dynamic_update_slice_in_dim(full, going_up, (here - far) % ways * lap, axis=0)
+        if 2 * far < ways:
+            going_down = lax.ppermute(
+                going_down, "tensor", [(d, (d - 1) % ways) for d in range(ways)]
+            )
+            full = lax.dynamic_update_slice_in_dim(
+                full, going_down, (here + far) % ways * lap, axis=0
+            )
+    gathered = full
     group_rows = gathered.shape[0]
     num_blocks = group_rows // BLK
     seq_blocks = min(4, num_blocks // 2)

time: 760 us -> 786 us (1.034)
  waiting for transfers between devices: 378 us -> 389 us
  starting transfers between devices: 0.96 us -> 10.4 us
  local copies, waits for them, and re-layouts: 53.6 us -> 61.8 us
    ppermute x0 -> x3, waiting for transfers between devices: none -> 38 us  [the longest x2 38 us: shards(): lax.ppermute(going_up, 'tensor', [(d, (d + 1) % ways) for d in range(ways)])]
    all_gather x1 -> x0, waiting for transfers between devices: 29.4 us -> none  [shards(): gathered = lax.all_gather(normed_low, 'tensor', axis=0, tiled=True)]
    ppermute x0 -> x3, starting transfers between devices: none -> 9.51 us  [the longest x2 7.59 us: shards(): lax.ppermute(going_up, 'tensor', [(d, (d + 1) % ways) for d in range(ways)])]
  transfers between devices with their start and end apart: 8 -> 10, of which waited for: 6 -> 7; matrix products, arithmetic and copies ran while one was open for 21% -> 21% of each run, Pallas kernels for 0% -> 0%
where the time goes in v1:
time: 786 us; the launch traced here: 781 us
  waiting for transfers between devices  389 us (49%)
  matrix products  185 us (24%)
  other arithmetic  67.8 us (9%)
  local copies, waits for them, and re-layouts  61.8 us (8%)
  blocking collectives  40.9 us (5%)
  between operations  14.9 us (2%)
  loops' own time  10.9 us (1%)
  starting transfers between devices  10.4 us (1%)
    reduce_scatter x1, waiting for transfers between devices, shards(): lax.psum_scatter(grad_w_down, 'dp', scatter_dimension=1, tiled=True)  92.6 us
    reduce_scatter x1, waiting for transfers between devices, shards(): lax.psum_scatter(grad_w_in_local, 'dp', scatter_dimension=0, tiled=True)  91.5 us
    reduce_scatter x1, waiting for transfers between devices, shards(): lax.psum_scatter(grad_w_qkv_local, 'dp', scatter_dimension=1, tiled=True)  77.9 us
    reduce_scatter x1, waiting for transfers between devices, shards(): lax.psum_scatter(jnp.dot(attended, w_out_flat, preferred_element_type=jnp...  66.7 us
    psum x1, blocking collectives, shards(): lax.psum((grad_gain_part, grad_bias_part, grad_bout_part, bqkv_full, bin_...  40.9 us
    ppermute x2, waiting for transfers between devices, shards(): lax.ppermute(going_up, 'tensor', [(d, (d + 1) % ways) for d in range(ways)])  38 us
    dot_general x1, matrix products, shards(): jnp.einsum('td,fd->tf', cotangent_group, w_down, preferred_element_type=j...  26.8 us
    reduce_scatter x1, waiting for transfers between devices, shards(): lax.psum_scatter(grad_w_out.reshape(heads_local, head_dim, model_width),...  22.6 us
  transfers between devices with their start and end apart: 10, of which 7 were waited for; matrix products, arithmetic and copies ran while one was open for 21% of the time, Pallas kernels for 0%

profile of v1, /device:TPU:0, one launch (start us, length us, event | category | flops | bytes accessed | tf_op | source)
XLA Modules:
  0.0 781.5 jit_solution(5258973032276454416)
XLA Ops:
  24.6 23.1 %collective-permute-done = bf16[512,1024]{1,0:T(8,128)(2,1)} collective-permute-done((bf16[512,1024]{1,0:T(8,128)(2,1)}, bf16[512,1024]{1,0:T(8,128)(2,1)}, u32[]{:S(2)}, u32[]{:S(2)}) %collective-permute-start) | collective-permute-done | bytes 1048608 | tf_op jit(solution)/shard_map/ppermute | solution.py:60
  47.7 7.1 collective-permute-start.2
  60.3 14.9 %collective-permute-done.2 = bf16[512,1024]{1,0:T(8,128)(2,1)S(1)} collective-permute-done((bf16[512,1024]{1,0:T(8,128)(2,1)}, bf16[512,1024]{1,0:T(8,128)(2,1)S(1)}, u32[]{:S(2)}, u32[]{:S(2)}) %collective-permute-start.2) | collective-permute-done | bytes 1048608 | tf_op jit(solution)/shard_map/ppermute | solution.py:60
  76.3 13.9 %convolution_add_fusion = f32[2048,1792]{0,1:T(8,128)} fusion(bf16[2048,1024]{1,0:T(8,128)(2,1)} %constant_dynamic-update-slice_fusion.1, f32[1792]{0:T(1024)S(1)} %pad_maximum_fusion.8, bf16[1024,1024]{1,0:T(8,128)(2,1)S(1)} %copy-done.38, bf16[1024,256]{1,0:T(8,128)(2,1)S(1)} %copy-done.22, bf16[1024,256]{1,0:T(8,128)(2,1)S(1)} %copy-done.20, ...), kind=kOutput, calls=%fused_computation.77 | convolution fusion | flops 7534542848 | bytes 22551552 | tf_op jit(solution)/shard_map/dot_general | solution.py:85
  90.2 2.5 fusion.89
  98.4 59.7 %while.31 = (s32[]{:T(128)}, bf16[4,512,4,64]{1,3,2,0:T(8,128)(2,1)}, f32[4,4,512]{2,1,0:T(4,128)}, s32[4]{0:T(128)S(1)}, bf16[2560,4,64]{0,2,1:T(8,128)(2,1)}, ...) while((s32[]{:T(128)}, ...), condition=%wide.region_6.7_spmd.clone, body=%wide.region_3.6_spmd.clone.sunk | while | flops 563084288 | bytes 29175080 | solution.py:133
  103.3 2.8 fusion.129
  109.0 4.3 fusion.131
  118.2 2.8 fusion.129
  123.9 4.3 fusion.131
  133.1 2.8 fusion.129
  138.9 4.3 fusion.131
  148.0 2.8 fusion.129
  153.8 4.3 fusion.131
  158.1 4.5 convolution_convert_fusion
  167.8 80.2 %while.32 = (s32[]{:T(128)}, f32[2048,4,64]{0,2,1:T(8,128)}, f32[2560,4,64]{0,2,1:T(8,128)}, f32[2560,4,64]{0,2,1:T(8,128)}, bf16[2560,4,64]{0,2,1:T(8,128)(2,1)...) while((s32[]{:T(128)}, f32[2048,4,64]{0,2,1:T(8,128)}, ...), condition=%wide.region_10.11_spmd.clone, body=%wide.region_8.10_spmd.clone.sunk | while | flops 1375599616 | bytes 97585616 | solution.py:203
  172.8 4.2 multiply_reduce_fusion.2
  177.0 2.4 multiply_convert_fusion.3
  183.5 4.5 fusion.144
  192.8 4.2 multiply_reduce_fusion.2
  197.0 2.4 multiply_convert_fusion.3
  203.5 4.5 fusion.144
  212.7 4.2 multiply_reduce_fusion.2
  216.9 2.4 multiply_convert_fusion.3
  223.5 4.5 fusion.144
  232.7 4.2 multiply_reduce_fusion.2
  243.5 4.5 fusion.144
  254.6 26.8 %add_convert_fusion = (bf16[2048,1024]{0,1:T(8,128)(2,1)S(1)}, f32[2048,1024]{0,1:T(8,128)}) fusion(f32[2048,1792]{0,1:T(8,128)} %convolution_add_fusion, bf16[2048,1024]{1,0:T(8,128)(2,1)S(1)} %copy-done.37, bf16[1024,1024]{1,0:T(8,128)(2,1)S(1)} %copy-done), kind=kOutput, calls=%fused_computation.61 | convolution fusion | flops 4445962240 | bytes 27262976 | tf_op jit(solution)/shard_map/td,fd->tf/dot_general | solution.py:153
  283.3 12.7 %fusion.79 = f32[2048,1024]{1,0:T(8,128)} fusion(bf16[1024,1024]{1,0:T(8,128)(2,1)} %param.21, bf16[1024,256]{1,0:T(8,128)(2,1)S(1)} %copy-done.23, bf16[1024,256]{1,0:T(8,128)(2,1)S(1)} %copy-done.21, bf16[1024,256]{1,0:T(8,128)(2,1)S(1)} %copy-done.19, bf16[2048,1024]{0,1:T(8,128)(2,1)S(1)} %get-tuple-element.373, bf16[2048,256]{0,1:T(8,128)(2,1)S(1)} %bitcast.104, ...), kind=kOutput, calls=%fused_computation.119 | convolution fusion | flops 7560232960 | bytes 19398656 | tf_op jit(solution)/shard_map/tc,dc->td/dot_general | solution.py:225
  298.6 11.4 %multiply_convert_fusion.1 = bf16[2048,1024]{0,1:T(8,128)(2,1)} fusion(f32[2048,1024]{0,1:T(8,128)} %get-tuple-element.374, f32[2048,1792]{0,1:T(8,128)} %convolution_add_fusion), kind=kLoop, calls=%fused_computation.62 | loop fusion | flops 6291456 | bytes 20971520 | tf_op jit(solution)/shard_map/convert_element_type | solution.py:137
  310.0 7.0 fusion.92
  317.0 4.8 convolution_add_fusion.1
  321.9 4.4 fusion.59
  326.6 12.1 %fusion.85 = f32[1024,1792]{1,0:T(8,128)S(1)} fusion(bf16[2048,1024]{1,0:T(8,128)(2,1)} %constant_dynamic-update-slice_fusion.1, bf16[2048,1024]{0,1:T(8,128)(2,1)} %copy-done.8, bf16[2048,256]{0,1:T(8,128)(2,1)} %bitcast.105, bf16[2048,256]{0,1:T(8,128)(2,1)} %bitcast.114, bf16[2048,256]{0,1:T(8,128)(2,1)} %bitcast.111), kind=kOutput, calls=%fused_computation.153 | convolution fusion | flops 7545552896 | bytes 18874368 | tf_op jit(solution)/shard_map/td,tc->dc/dot_general | solution.py:220
  338.8 3.0 copy-done.7
  345.1 2.5 copy.41
  347.7 2.6 copy.42
  350.2 3.7 pad_maximum_fusion.2
  354.0 4.8 slice.139
  359.1 10.0 %fusion.93 = f32[1024,1024]{1,0:T(8,128)} fusion(bf16[2048,1024]{0,1:T(8,128)(2,1)} %multiply_convert_fusion.1, bf16[2048,1024]{1,0:T(8,128)(2,1)} %all-gather.2.cloned.1.call-done), kind=kOutput, calls=%fused_computation.159 | convolution fusion | flops 4294967296 | bytes 12582912 | tf_op jit(solution)/shard_map/tf,td->fd/dot_general | solution.py:159
  369.2 4.3 convert_reduce_fusion
  377.0 66.7 %reduce-scatter.7.cloned.1.call-done = f32[512,1024]{1,0:T(8,128)} async-done(((f32[2048,1024]{1,0:T(8,128)}), f32[512,1024]{1,0:T(8,128)}) %reduce-scatter.7.cloned.1.call-update) | async-done | bytes 2097168 | tf_op jit(solution)/shard_map/reduce_scatter | solution.py:141
  443.7 5.1 convert_reduce_fusion.2
  448.9 40.9 %all-reduce.2 = (f32[1024]{0:T(1024)}, f32[1024]{0:T(1024)}, f32[3,16,64]{2,1,0:T(8,128)}, f32[4096]{0:T(1024)}, f32[1024]{0:T(1024)}) all-reduce(f32[1024]{0:T(1024)S(1)} %get-tuple-element.320, f32[1024]{0:T(1024)S(1)} %get-tuple-element.322, ...), channel_id=1, replica_groups=mesh['dp'=8,'tensor'=4] {'dp','tensor'}, use_global_device_ids=true, to_apply=%region_15.16 | all-reduce | flops 10240 | bytes 81920 | tf_op jit(solution)/shard_map/psum | solution.py:253
  489.8 22.6 %reduce-scatter.15.cloned.1.call-done = f32[4,64,128]{2,1,0:T(8,128)} async-done(((f32[4,64,1024]{2,1,0:T(8,128)}), f32[4,64,128]{2,1,0:T(8,128)}) %reduce-scatter.15.cloned.1.call-update) | async-done | bytes 131088 | tf_op jit(solution)/shard_map/reduce_scatter | solution.py:259
  512.4 77.9 %reduce-scatter.11.cloned.1.call-done = f32[3,128,4,64]{1,3,2,0:T(8,128)} async-done(((f32[3,1024,4,64]{1,3,2,0:T(8,128)}), f32[3,128,4,64]{1,3,2,0:T(8,128)}) %reduce-scatter.11.cloned.1.call-update) | async-done | bytes 393232 | tf_op jit(solution)/shard_map/reduce_scatter | solution.py:257
  590.3 91.5 %reduce-scatter.13.cloned.1.call-done = f32[128,1024]{1,0:T(8,128)} async-done(((f32[1024,1024]{1,0:T(8,128)}), f32[128,1024]{1,0:T(8,128)}) %reduce-scatter.13.cloned.1.call-update) | async-done | bytes 524304 | tf_op jit(solution)/shard_map/reduce_scatter | solution.py:258
  681.8 92.6 %reduce-scatter.17.cloned.1.call-done = f32[1024,128]{1,0:T(8,128)} async-done(((f32[1024,1024]{1,0:T(8,128)}), f32[1024,128]{1,0:T(8,128)}) %reduce-scatter.17.cloned.1.call-update) | async-done | bytes 524304 | tf_op jit(solution)/shard_map/reduce_scatter | solution.py:265
  (235 shorter events, 111.9 us)
Async XLA Ops:
  7.2 247.3 %copy-start = (bf16[1024,1024]{1,0:T(8,128)(2,1)S(1)}, bf16[1024,1024]{1,0:T(8,128)(2,1)}, u32[]{:S(2)}) copy-start(bf16[1024,1024]{1,0:T(8,128)(2,1)} %param.24) | copy-start | bytes 6291460
  7.2 4.5 copy-start.2
  7.2 4.5 copy-start.27
  7.2 4.5 copy-start.34
  7.2 150.9 %all-gather.2.cloned.1.call-start = ((), (), s32[]{:S(2)}) async-start(), calls=%async_computation.7 | async-start | bytes 5242880 | tf_op jit(solution)/shard_map/all_gather | solution.py:149
  8.9 4.2 copy-start.25
  11.1 6.5 copy-start.29
  11.1 6.6 copy-start.39
  15.2 9.2 %copy-start.33 = (f32[3,4,64]{2,1,0:T(4,128)S(1)}, f32[3,4,64]{2,1,0:T(4,128)}, u32[]{:S(2)}) copy-start(f32[3,4,64]{2,1,0:T(4,128)} %param.20) | copy-start | bytes 9220
  15.2 9.4 %copy-start.36 = (f32[1024]{0:T(1024)S(1)}, f32[1024]{0:T(1024)}, u32[]{:S(2)}) copy-start(f32[1024]{0:T(1024)} %param.22) | copy-start | bytes 12292
  15.2 32.5 %collective-permute-start = (bf16[512,1024]{1,0:T(8,128)(2,1)}, bf16[512,1024]{1,0:T(8,128)(2,1)}, u32[]{:S(2)}, u32[]{:S(2)}) collective-permute-start(bf16[512,1024]{1,0:T(8,128)(2,1)} %get-tuple-element.376), channel_id=1, source_target_pairs={{0,1},{1,2},{2,3},{3,0},{4,5},{5,6},{6,7},{7,4},{8,9},{9,10},{10,1... | collective-permute-start | bytes 3145736 | tf_op jit(solution)/shard_map/ppermute | solution.py:60
  15.7 42.4 %collective-permute-start.1 = (bf16[512,1024]{1,0:T(8,128)(2,1)}, bf16[512,1024]{1,0:T(8,128)(2,1)}, u32[]{:S(2)}, u32[]{:S(2)}) collective-permute-start(bf16[512,1024]{1,0:T(8,128)(2,1)} %get-tuple-element.376), channel_id=1, source_target_pairs={{0,3},{1,0},{2,1},{3,2},{4,7},{5,4},{6,5},{7,6},{8,11},{9,8},{10,9... | collective-permute-start | bytes 3145736 | tf_op jit(solution)/shard_map/ppermute | solution.py:63
  17.6 356.0 %reduce-scatter.9.cloned.1.call-start = ((), (), s32[]{:S(2)}) async-start(), calls=%async_computation.8 | async-start | bytes 10485760 | tf_op jit(solution)/shard_map/reduce_scatter | solution.py:224
  23.4 52.9 %copy-start.18 = (bf16[1024,256]{1,0:T(8,128)(2,1)S(1)}, bf16[1024,256]{1,0:T(8,128)(2,1)}, u32[]{:S(2)}) copy-start(bf16[1024,256]{1,0:T(8,128)(2,1)} %copy.36) | copy-start | bytes 1572868
  24.4 51.9 %copy-start.20 = (bf16[1024,256]{1,0:T(8,128)(2,1)S(1)}, bf16[1024,256]{1,0:T(8,128)(2,1)}, u32[]{:S(2)}) copy-start(bf16[1024,256]{1,0:T(8,128)(2,1)} %copy.37) | copy-start | bytes 1572868
  24.6 51.7 %copy-start.22 = (bf16[1024,256]{1,0:T(8,128)(2,1)S(1)}, bf16[1024,256]{1,0:T(8,128)(2,1)}, u32[]{:S(2)}) copy-start(bf16[1024,256]{1,0:T(8,128)(2,1)} %copy.38) | copy-start | bytes 1572868
  24.6 51.7 %copy-start.38 = (bf16[1024,1024]{1,0:T(8,128)(2,1)S(1)}, bf16[1024,1024]{1,0:T(8,128)(2,1)}, u32[]{:S(2)}) copy-start(bf16[1024,1024]{1,0:T(8,128)(2,1)} %param.21) | copy-start | bytes 6291460
  47.7 27.5 %collective-permute-start.2 = (bf16[512,1024]{1,0:T(8,128)(2,1)}, bf16[512,1024]{1,0:T(8,128)(2,1)S(1)}, u32[]{:S(2)}, u32[]{:S(2)}) collective-permute-start(bf16[512,1024]{1,0:T(8,128)(2,1)} %collective-permute-done), channel_id=1, source_target_pairs={{0,1},{1,2},{2,3},{3,0},{4,5},{5,6},{6,7},{7,4},{8,9},{9,10},{10,1... | collective-permute-start | bytes 3145736 | tf_op jit(solution)/shard_map/ppermute | solution.py:60
  55.8 40.2 %copy-start.14 = (f32[2048,8]{0,1:T(8,128)}, f32[2048,8]{0,1:T(8,128)S(1)}, u32[]{:S(2)}) copy-start(f32[2048,8]{0,1:T(8,128)S(1)} %get-tuple-element.406) | copy-start | bytes 196612
  98.4 59.7 %copy-start.16 = (bf16[4,64,1024]{2,1,0:T(8,128)(2,1)S(1)}, bf16[4,64,1024]{2,1,0:T(8,128)(2,1)}, u32[]{:S(2)}) copy-start(bf16[4,64,1024]{2,1,0:T(8,128)(2,1)} %param.23) | copy-start | bytes 1572868
  162.6 5.2 copy-start.1
  167.8 83.2 %copy-start.15 = (f32[2048,8]{0,1:T(8,128)S(1)}, f32[2048,8]{0,1:T(8,128)}, u32[]{:S(2)}) copy-start(f32[2048,8]{0,1:T(8,128)} %copy-done.14) | copy-start | bytes 196612
  167.8 83.3 %copy-start.24 = (f32[2048,8]{0,1:T(8,128)S(1)}, f32[2048,8]{0,1:T(8,128)}, u32[]{:S(2)}) copy-start(f32[2048,8]{0,1:T(8,128)} %get-tuple-element.404) | copy-start | bytes 196612
  168.0 4.8 copy-start.13
  177.0 2.4 copy-start.4
  188.0 4.7 copy-start.13
  208.0 4.7 copy-start.13
  228.0 4.7 copy-start.13
  251.0 3.5 copy-start.37
  254.3 27.0 %copy-start.10 = (bf16[2048,4,64]{0,2,1:T(8,128)(2,1)}, bf16[2048,4,64]{0,2,1:T(8,128)(2,1)S(1)}, u32[]{:S(2)}) copy-start(bf16[2048,4,64]{0,2,1:T(8,128)(2,1)S(1)} %slice.174) | copy-start | bytes 3145732
  254.5 26.8 %copy-start.11 = (bf16[2048,4,64]{0,2,1:T(8,128)(2,1)}, bf16[2048,4,64]{0,2,1:T(8,128)(2,1)S(1)}, u32[]{:S(2)}) copy-start(bf16[2048,4,64]{0,2,1:T(8,128)(2,1)S(1)} %get-tuple-element.407) | copy-start | bytes 3145732
  254.5 26.8 %copy-start.12 = (bf16[2048,4,64]{0,2,1:T(8,128)(2,1)}, bf16[2048,4,64]{0,2,1:T(8,128)(2,1)S(1)}, u32[]{:S(2)}) copy-start(bf16[2048,4,64]{0,2,1:T(8,128)(2,1)S(1)} %get-tuple-element.408) | copy-start | bytes 3145732
  254.5 28.8 %copy-start.19 = (bf16[1024,256]{1,0:T(8,128)(2,1)S(1)}, bf16[1024,256]{1,0:T(8,128)(2,1)}, u32[]{:S(2)}) copy-start(bf16[1024,256]{1,0:T(8,128)(2,1)} %copy.36) | copy-start | bytes 1572868
  254.6 28.8 %copy-start.21 = (bf16[1024,256]{1,0:T(8,128)(2,1)S(1)}, bf16[1024,256]{1,0:T(8,128)(2,1)}, u32[]{:S(2)}) copy-start(bf16[1024,256]{1,0:T(8,128)(2,1)} %copy.37) | copy-start | bytes 1572868
  254.6 28.8 %copy-start.23 = (bf16[1024,256]{1,0:T(8,128)(2,1)S(1)}, bf16[1024,256]{1,0:T(8,128)(2,1)}, u32[]{:S(2)}) copy-start(bf16[1024,256]{1,0:T(8,128)(2,1)} %copy.38) | copy-start | bytes 1572868
  296.1 147.6 %reduce-scatter.7.cloned.1.call-start = ((), (), s32[]{:S(2)}) async-start(), calls=%async_computation.6 | async-start | bytes 10485760 | tf_op jit(solution)/shard_map/reduce_scatter | solution.py:141
  310.0 7.0 copy-start.17
  321.8 190.5 %reduce-scatter.15.cloned.1.call-start = ((), (), s32[]{:S(2)}) async-start(), calls=%async_computation.11 | async-start | bytes 1179648 | tf_op jit(solution)/shard_map/reduce_scatter | solution.py:259
  326.3 263.9 %reduce-scatter.11.cloned.1.call-start = ((), (), s32[]{:S(2)}) async-start(), calls=%async_computation.9 | async-start | bytes 3538944 | tf_op jit(solution)/shard_map/reduce_scatter | solution.py:257
  338.8 3.0 copy-start.7
  353.9 327.9 %reduce-scatter.13.cloned.1.call-start = ((), (), s32[]{:S(2)}) async-start(), calls=%async_computation.10 | async-start | bytes 4718592 | tf_op jit(solution)/shard_map/reduce_scatter | solution.py:258
  358.8 415.6 %reduce-scatter.17.cloned.1.call-start = ((), (), s32[]{:S(2)}) async-start(), calls=%async_computation.12 | async-start | bytes 4718592 | tf_op jit(solution)/shard_map/reduce_scatter | solution.py:265
  369.1 4.5 copy-start.3
  369.1 4.5 copy-start.26
  369.1 4.5 copy-start.28
  369.1 6.8 copy-start.32
  369.2 6.8 copy-start.30
  373.5 70.2 %copy-start.35 = (f32[1024]{0:T(1024)S(1)}, f32[1024]{0:T(1024)}, u32[]{:S(2)}) copy-start(f32[1024]{0:T(1024)} %param.25) | copy-start | bytes 12292
  (15 other events, 32.3 us)
Sparse Core Ops, SparseCore 0:
  17.8 53.6 all-gather.1
  296.2 73.4 reduce-scatter.8
  372.3 71.4 reduce-scatter.6
  447.6 64.7 reduce-scatter.14
  516.4 73.8 reduce-scatter.10
  594.3 87.4 reduce-scatter.12
  686.0 88.3 reduce-scatter.16
